TPU v7x, 32 devices: a whole 2x2x4 slice. The times are simulated.
32 devices in a mesh: seq: 4 (over y, x), fsdp: 8 (over z, core).
Axes of the slice: x: 2, y: 2, z: 4, core: 2. Of those that a mesh axis runs over, the one named last changes fastest.
Arguments:
- layer_in: float32 [2, 4, 1024, 2048], P(None, 'seq', 'fsdp'), may hold values from -6 to 6
- doc_ids: int32 [2, 4, 1024], P(None, 'seq'), may hold values from 0 to 3, as said below
- out_grad: float32 [2, 4, 1024, 2048], P(None, 'seq', 'fsdp'), may hold values from -6 to 6
- query_weight: float32 [2048, 2048], P(('seq', 'fsdp')), may hold values from -0.125 to 0.125
- query_bias: float32 [2048], P(('seq', 'fsdp')), may hold values from -3 to 3
- key_weight: float32 [2048, 2048], P(('seq', 'fsdp')), may hold values from -0.1875 to 0.1875
- value_weight: float32 [2048, 2048], P(('seq', 'fsdp')), may hold values from -0.125 to 0.125
- value_bias: float32 [2048], P(('seq', 'fsdp')), may hold values from -2 to 2
- output_weight: float32 [2048, 2048], P(('seq', 'fsdp')), may hold values from -2 to 2
- output_bias: float32 [2048], P(('seq', 'fsdp')), may hold values from -3 to 3
- first_gain: float32 [2048], P(('seq', 'fsdp')), may hold values from 0.25 to 1.75
- first_shift: float32 [2048], P(('seq', 'fsdp')), may hold values from -2 to 2
- up_weight: float32 [2048, 8192], P(('seq', 'fsdp')), may hold values from -0.125 to 0.125
- up_bias: float32 [8192], P(('seq', 'fsdp')), may hold values from -3 to 3
- down_weight: float32 [8192, 2048], P(('seq', 'fsdp')), may hold values from -0.0625 to 0.0625
- down_bias: float32 [2048], P(('seq', 'fsdp')), may hold values from -3 to 3
- second_gain: float32 [2048], P(('seq', 'fsdp')), may hold values from 0.25 to 1.75
- second_shift: float32 [2048], P(('seq', 'fsdp')), may hold values from -2 to 2
Outputs:
- layer_out: float32 [2, 4, 1024, 2048], P(None, 'seq', 'fsdp')
- input_grad: float32 [2, 4, 1024, 2048], P(None, 'seq', 'fsdp')
- query_weight_grad: float32 [2048, 2048], P(('seq', 'fsdp'))
- query_bias_grad: float32 [2048], P(('seq', 'fsdp'))
- key_weight_grad: float32 [2048, 2048], P(('seq', 'fsdp'))
- value_weight_grad: float32 [2048, 2048], P(('seq', 'fsdp'))
- value_bias_grad: float32 [2048], P(('seq', 'fsdp'))
- output_weight_grad: float32 [2048, 2048], P(('seq', 'fsdp'))
- output_bias_grad: float32 [2048], P(('seq', 'fsdp'))
- first_gain_grad: float32 [2048], P(('seq', 'fsdp'))
- first_shift_grad: float32 [2048], P(('seq', 'fsdp'))
- up_weight_grad: float32 [2048, 8192], P(('seq', 'fsdp'))
- up_bias_grad: float32 [8192], P(('seq', 'fsdp'))
- down_weight_grad: float32 [8192, 2048], P(('seq', 'fsdp'))
- down_bias_grad: float32 [2048], P(('seq', 'fsdp'))
- second_gain_grad: float32 [2048], P(('seq', 'fsdp'))
- second_shift_grad: float32 [2048], P(('seq', 'fsdp'))
Inputs may be any that keep to these rules, and one draw needn't show every extreme that they name: `doc_ids`: within a sequence the document numbers never fall, every one of the 4 numbers occurs, and each document holds 102 to 718 tokens; in every draw some sequence has a document of exactly 718 tokens.
All inputs are finite; a program needn't handle non-finite values.
Results may differ from a plain program's by a relative error of at most 0.015.
The roundings to bfloat16 on the way count: a program that leaves them out, or rounds other values in their place, can miss the bound.
Values may be sent and summed in bfloat16 or wider, within the bound.
No kernel may reach another device: no remote copies, remote signals or barrier semaphores. Data moves between devices by JAX's collectives and lax.ppermute only.
A program may use at most 512 MiB of HBM per device.

v0:
```python
from functools import reduce
import jax
import jax.numpy as jnp
from jax import lax
from jax.sharding import PartitionSpec as P

D = 2048
H = 16
DH = 128
MB = 2
norm_eps = 1e-06
masked_score = -1e30


def normalize_forward(summed, gain_vector, shift_vector):
    center = summed - jnp.mean(summed, axis=-1, keepdims=True)
    inverse = lax.rsqrt(jnp.mean(center * center, axis=-1, keepdims=True) + norm_eps)
    normed = center * inverse
    return (normed * gain_vector + shift_vector, normed, inverse)


def normalize_backward(grad_output, normed, inverse, gain_vector):
    grad_normed = grad_output * gain_vector
    centered = grad_normed - jnp.mean(grad_normed, axis=-1, keepdims=True)
    grad_input = inverse * (
        centered - normed * jnp.mean(grad_normed * normed, axis=-1, keepdims=True)
    )
    return (grad_input, jnp.sum(grad_output * normed, axis=0), jnp.sum(grad_output, axis=0))


def masked_scores(query_heads, key_heads, row_ids, all_ids, score_scale):
    scores = (
        jnp.einsum("thd,shd->hts", query_heads, key_heads, preferred_element_type=jnp.float32)
        * score_scale
    )
    same_doc = row_ids[:, None] == all_ids[None, :]
    return jnp.where(same_doc[None], scores, masked_score)


def matmul(left, right):
    return jnp.dot(left, right, preferred_element_type=jnp.float32)


def transposed(left, right):
    return jnp.einsum("ti,tj->ij", left, right, preferred_element_type=jnp.float32)


def against(left, right):
    return jnp.einsum("ti,ji->tj", left, right, preferred_element_type=jnp.float32)


def gelu_tanh(argument):
    return jax.nn.gelu(argument, approximate=True)


def column_sum(matrix):
    return jnp.sum(matrix.astype(jnp.float32), axis=0)


def weight_terms(factors, norm_terms):
    (
        rounded_in,
        grad_query,
        grad_key,
        grad_value,
        mixed_rows,
        grad_branch,
        hidden_low,
        grad_up,
        active_low,
        grad_down,
    ) = factors
    first_gain_part, first_shift_part, second_gain_part, second_shift_part = norm_terms
    return (
        transposed(rounded_in, grad_query),
        column_sum(grad_query),
        transposed(rounded_in, grad_key),
        transposed(rounded_in, grad_value),
        column_sum(grad_value),
        transposed(mixed_rows, grad_branch),
        column_sum(grad_branch),
        first_gain_part,
        first_shift_part,
        transposed(hidden_low, grad_up),
        column_sum(grad_up),
        transposed(active_low, grad_down),
        column_sum(grad_down),
        second_gain_part,
        second_shift_part,
    )


def shards(
    layer_in,
    doc_ids,
    out_grad,
    query_weight,
    query_bias,
    key_weight,
    value_weight,
    value_bias,
    output_weight,
    output_bias,
    first_gain,
    first_shift,
    up_weight,
    up_bias,
    down_weight,
    down_bias,
    second_gain,
    second_shift,
):
    low_type = jnp.bfloat16
    wide_type = jnp.float32
    local = (
        query_weight.astype(low_type),
        query_bias.astype(low_type),
        key_weight.astype(low_type),
        value_weight.astype(low_type),
        value_bias.astype(low_type),
        output_weight.astype(low_type),
        output_bias.astype(low_type),
        first_gain.astype(low_type),
        first_shift.astype(low_type),
        up_weight.astype(low_type),
        up_bias.astype(low_type),
        down_weight.astype(low_type),
        down_bias.astype(low_type),
        second_gain.astype(low_type),
        second_shift.astype(low_type),
    )
    tokens_here = layer_in.shape[2]
    start_row = lax.axis_index("fsdp") * tokens_here
    score_scale = DH ** (-0.5)
    outputs = []
    input_grads = []
    grad_total = None
    stored_factors = []
    stored_norms = []
    (
        query_matrix,
        query_offset,
        key_matrix,
        value_matrix,
        value_offset,
        output_matrix,
        output_offset,
        first_scale,
        first_offset,
        up_matrix,
        up_offset,
        down_matrix,
        down_offset,
        second_scale,
        second_offset,
    ) = (
        lax.all_gather(local[0], ("seq", "fsdp"), axis=0, tiled=True),
        lax.all_gather(local[1], ("seq", "fsdp"), axis=0, tiled=True),
        lax.all_gather(local[2], ("seq", "fsdp"), axis=0, tiled=True),
        lax.all_gather(local[3], ("seq", "fsdp"), axis=0, tiled=True),
        lax.all_gather(local[4], ("seq", "fsdp"), axis=0, tiled=True),
        lax.all_gather(local[5], ("seq", "fsdp"), axis=0, tiled=True),
        lax.all_gather(local[6], ("seq", "fsdp"), axis=0, tiled=True),
        lax.all_gather(local[7], ("seq", "fsdp"), axis=0, tiled=True),
        lax.all_gather(local[8], ("seq", "fsdp"), axis=0, tiled=True),
        lax.all_gather(local[9], ("seq", "fsdp"), axis=0, tiled=True),
        lax.all_gather(local[10], ("seq", "fsdp"), axis=0, tiled=True),
        lax.all_gather(local[11], ("seq", "fsdp"), axis=0, tiled=True),
        lax.all_gather(local[12], ("seq", "fsdp"), axis=0, tiled=True),
        lax.all_gather(local[13], ("seq", "fsdp"), axis=0, tiled=True),
        lax.all_gather(local[14], ("seq", "fsdp"), axis=0, tiled=True),
    )
    for portion in range(MB):
        inputs = layer_in[portion, 0]
        all_ids = doc_ids[portion, 0]
        row_ids = lax.dynamic_slice_in_dim(all_ids, start_row, tokens_here)
        rounded_in = inputs.astype(low_type)
        query_rows = (matmul(rounded_in, query_matrix) + query_offset.astype(wide_type)).astype(
            low_type
        )
        key_rows = matmul(rounded_in, key_matrix).astype(low_type)
        value_rows = (matmul(rounded_in, value_matrix) + value_offset.astype(wide_type)).astype(
            low_type
        )
        key_whole, value_whole = (
            lax.all_gather(key_rows, "fsdp", axis=0, tiled=True),
            lax.all_gather(value_rows, "fsdp", axis=0, tiled=True),
        )
        length = key_whole.shape[0]
        query_heads = query_rows.reshape(tokens_here, H, DH)
        key_heads = key_whole.reshape(length, H, DH)
        value_heads = value_whole.reshape(length, H, DH)
        scores = masked_scores(query_heads, key_heads, row_ids, all_ids, score_scale)
        row_max = jnp.max(scores, axis=-1, keepdims=True)
        log_total = row_max + jnp.log(jnp.sum(jnp.exp(scores - row_max), axis=-1, keepdims=True))
        attend_low = jnp.exp(scores - log_total).astype(low_type)
        mixed_rows = jnp.einsum(
            "hts,shd->thd", attend_low, value_heads, preferred_element_type=wide_type
        )
        mixed_rows = mixed_rows.reshape(tokens_here, D).astype(low_type)
        branch = matmul(mixed_rows, output_matrix) + output_offset.astype(wide_type)
        hidden, first_normed, first_inverse = normalize_forward(
            inputs + branch, first_scale.astype(wide_type), first_offset.astype(wide_type)
        )
        hidden_low = hidden.astype(low_type)
        up_rows = matmul(hidden_low, up_matrix) + up_offset.astype(wide_type)
        active, gelu_back = jax.vjp(gelu_tanh, up_rows)
        active_low = active.astype(low_type)
        down_rows = matmul(active_low, down_matrix) + down_offset.astype(wide_type)
        result, second_normed, second_inverse = normalize_forward(
            hidden + down_rows, second_scale.astype(wide_type), second_offset.astype(wide_type)
        )
        outputs.append(result)
        (
            query_back,
            key_back,
            value_back,
            output_back,
            first_back,
            up_back,
            down_back,
            second_back,
        ) = (
            query_matrix,
            key_matrix,
            value_matrix,
            output_matrix,
            first_scale,
            up_matrix,
            down_matrix,
            second_scale,
        )
        grad_output = out_grad[portion, 0]
        grad_second, second_gain_part, second_shift_part = normalize_backward(
            grad_output, second_normed, second_inverse, second_back.astype(wide_type)
        )
        grad_down = grad_second.astype(low_type)
        grad_active = against(grad_down, down_back)
        grad_up = gelu_back(grad_active)[0].astype(low_type)
        grad_hidden = grad_second + against(grad_up, up_back)
        grad_first, first_gain_part, first_shift_part = normalize_backward(
            grad_hidden, first_normed, first_inverse, first_back.astype(wide_type)
        )
        grad_branch = grad_first.astype(low_type)
        grad_mixed = against(grad_branch, output_back).astype(low_type)
        grad_heads = grad_mixed.reshape(tokens_here, H, DH)
        scores = masked_scores(query_heads, key_heads, row_ids, all_ids, score_scale)
        attend = jnp.exp(scores - log_total)
        grad_attend = jnp.einsum(
            "thd,shd->hts", grad_heads, value_heads, preferred_element_type=wide_type
        )
        row_dot = jnp.sum(attend * grad_attend, axis=-1, keepdims=True)
        grad_scores = (attend * (grad_attend - row_dot)).astype(low_type)
        grad_query = (
            jnp.einsum("hts,shd->thd", grad_scores, key_heads, preferred_element_type=wide_type)
            * score_scale
        )
        grad_query = grad_query.reshape(tokens_here, D).astype(low_type)
        key_part = (
            jnp.einsum("hts,thd->shd", grad_scores, query_heads, preferred_element_type=wide_type)
            * score_scale
        )
        value_part = jnp.einsum(
            "hts,thd->shd", attend.astype(low_type), grad_heads, preferred_element_type=wide_type
        )
        key_sum, value_sum = (
            lax.psum_scatter(
                key_part.reshape(length, D).astype(jnp.bfloat16),
                "fsdp",
                scatter_dimension=0,
                tiled=True,
            ).astype(jnp.float32),
            lax.psum_scatter(
                value_part.reshape(length, D).astype(jnp.bfloat16),
                "fsdp",
                scatter_dimension=0,
                tiled=True,
            ).astype(jnp.float32),
        )
        grad_key = key_sum.astype(low_type)
        grad_value = value_sum.astype(low_type)
        input_grads.append(
            grad_first
            + against(grad_query, query_back)
            + against(grad_key, key_back)
            + against(grad_value, value_back)
        )
        factors = (
            rounded_in,
            grad_query,
            grad_key,
            grad_value,
            mixed_rows,
            grad_branch,
            hidden_low,
            grad_up,
            active_low,
            grad_down,
        )
        norm_terms = (first_gain_part, first_shift_part, second_gain_part, second_shift_part)
        stored_factors.append(factors)
        stored_norms.append(norm_terms)
    joined = tuple(
        (jnp.concatenate([entry[index] for entry in stored_factors], axis=0) for index in range(10))
    )
    summed_norms = tuple(
        (reduce(jnp.add, [entry[index] for entry in stored_norms]) for index in range(4))
    )
    terms = weight_terms(joined, summed_norms)
    grad_total = (
        lax.psum_scatter(terms[0], ("seq", "fsdp"), scatter_dimension=0, tiled=True),
        lax.psum_scatter(terms[1], ("seq", "fsdp"), scatter_dimension=0, tiled=True),
        lax.psum_scatter(terms[2], ("seq", "fsdp"), scatter_dimension=0, tiled=True),
        lax.psum_scatter(terms[3], ("seq", "fsdp"), scatter_dimension=0, tiled=True),
        lax.psum_scatter(terms[4], ("seq", "fsdp"), scatter_dimension=0, tiled=True),
        lax.psum_scatter(terms[5], ("seq", "fsdp"), scatter_dimension=0, tiled=True),
        lax.psum_scatter(terms[6], ("seq", "fsdp"), scatter_dimension=0, tiled=True),
        lax.psum_scatter(terms[7], ("seq", "fsdp"), scatter_dimension=0, tiled=True),
        lax.psum_scatter(terms[8], ("seq", "fsdp"), scatter_dimension=0, tiled=True),
        lax.psum_scatter(terms[9], ("seq", "fsdp"), scatter_dimension=0, tiled=True),
        lax.psum_scatter(terms[10], ("seq", "fsdp"), scatter_dimension=0, tiled=True),
        lax.psum_scatter(terms[11], ("seq", "fsdp"), scatter_dimension=0, tiled=True),
        lax.psum_scatter(terms[12], ("seq", "fsdp"), scatter_dimension=0, tiled=True),
        lax.psum_scatter(terms[13], ("seq", "fsdp"), scatter_dimension=0, tiled=True),
        lax.psum_scatter(terms[14], ("seq", "fsdp"), scatter_dimension=0, tiled=True),
    )
    layer_out = jnp.stack(outputs)[:, None]
    input_grad = jnp.stack(input_grads)[:, None]
    return (
        layer_out,
        input_grad,
        grad_total[0],
        grad_total[1],
        grad_total[2],
        grad_total[3],
        grad_total[4],
        grad_total[5],
        grad_total[6],
        grad_total[7],
        grad_total[8],
        grad_total[9],
        grad_total[10],
        grad_total[11],
        grad_total[12],
        grad_total[13],
        grad_total[14],
    )


def solution(mesh):
    placed = (
        P(None, "seq", "fsdp", None),
        P(None, "seq", None),
        P(None, "seq", "fsdp", None),
        P(("seq", "fsdp"), None),
        P(("seq", "fsdp")),
        P(("seq", "fsdp"), None),
        P(("seq", "fsdp"), None),
        P(("seq", "fsdp")),
        P(("seq", "fsdp"), None),
        P(("seq", "fsdp")),
        P(("seq", "fsdp")),
        P(("seq", "fsdp")),
        P(("seq", "fsdp"), None),
        P(("seq", "fsdp")),
        P(("seq", "fsdp"), None),
        P(("seq", "fsdp")),
        P(("seq", "fsdp")),
        P(("seq", "fsdp")),
    )
    return jax.shard_map(
        shards,
        mesh=mesh,
        in_specs=placed,
        out_specs=(
            P(None, "seq", "fsdp", None),
            P(None, "seq", "fsdp", None),
            P(("seq", "fsdp"), None),
            P(("seq", "fsdp")),
            P(("seq", "fsdp"), None),
            P(("seq", "fsdp"), None),
            P(("seq", "fsdp")),
            P(("seq", "fsdp"), None),
            P(("seq", "fsdp")),
            P(("seq", "fsdp")),
            P(("seq", "fsdp")),
            P(("seq", "fsdp"), None),
            P(("seq", "fsdp")),
            P(("seq", "fsdp"), None),
            P(("seq", "fsdp")),
            P(("seq", "fsdp")),
            P(("seq", "fsdp")),
        ),
        check_vma=False,
    )
```

profile of v0, /device:TPU:0, one launch (start us, length us, event | category | flops | bytes accessed | tf_op | source)
XLA Modules:
  0.0 3573.6 jit_solution(3197997986055923323)
XLA Ops:
  14.5 77.2 %all-gather.18.cloned.1.call-done = bf16[2048,2048]{1,0:T(8,128)(2,1)} async-done(((bf16[64,2048]{1,0:T(8,128)(2,1)}), bf16[2048,2048]{1,0:T(8,128)(2,1)}) %all-gather.18.cloned.1.call-update) | async-done | bytes 8388624 | tf_op jit(solution)/shard_map/all_gather | solution.py:159
  104.9 40.1 %all-reduce.18 = (bf16[2048]{0:T(1024)(128)(2,1)S(1)}, bf16[2048]{0:T(1024)(128)(2,1)S(1)}, bf16[2048]{0:T(1024)(128)(2,1)S(1)}, bf16[2048]{0:T(1024)(128)(2,1)S...) all-reduce(bf16[2048]{0:T(1024)(128)(2,1)S(1)} %dynamic-update-slic, ...), channel_id=1, replica_groups=mesh['seq'=4,'fsdp'=8] {'seq','fsdp'}, use_global_device_ids=true, to_apply=%add | all-reduce | flops 16384 | bytes 65536
  145.0 26.3 all-gather.12.cloned.1.call-done
  187.3 50.1 %all-gather = bf16[32,1,256]{2,1,0:T(2,128)(2,1)S(1)} all-gather(bf16[1,1,256]{2,1,0:T(2,128)(2,1)S(1)} %reshape.277), channel_id=1, replica_groups=mesh['seq'=4,'fsdp'=8] {'seq','fsdp'}, dimensions={0}, use_global_device_ids=true | all-gather | bytes 16896 | tf_op jit(solution)/shard_map/all_gather | solution.py:167
  237.9 13.3 all-gather.16.cloned.1.call-done
  262.1 36.9 %all-gather.20.cloned.1.call-done = bf16[1024,2048]{1,0:T(8,128)(2,1)} async-done(((bf16[128,2048]{1,0:T(8,128)(2,1)}), bf16[1024,2048]{1,0:T(8,128)(2,1)}) %all-gather.20.cloned.1.call-update) | async-done | bytes 4194320 | tf_op jit(solution)/shard_map/all_gather | solution.py:186
  305.4 41.5 %all-gather.30.cloned.1.call-done = bf16[1024,2048]{1,0:T(8,128)(2,1)} async-done(((bf16[128,2048]{1,0:T(8,128)(2,1)}), bf16[1024,2048]{1,0:T(8,128)(2,1)}) %all-gather.30.cloned.1.call-update) | async-done | bytes 4194320 | tf_op jit(solution)/shard_map/all_gather | solution.py:186
  360.9 33.9 all-gather.28.cloned.1.call-done
  394.8 8.2 fusion.50
  403.0 71.5 %all-gather.22.cloned.1.call-done = bf16[2048,2048]{1,0:T(8,128)(2,1)} async-done(((bf16[64,2048]{1,0:T(8,128)(2,1)}), bf16[2048,2048]{1,0:T(8,128)(2,1)}) %all-gather.22.cloned.1.call-update) | async-done | bytes 8388624 | tf_op jit(solution)/shard_map/all_gather | solution.py:162
  485.2 37.3 %all-gather.14.cloned.1.call-done = bf16[1024,2048]{1,0:T(8,128)(2,1)} async-done(((bf16[128,2048]{1,0:T(8,128)(2,1)}), bf16[1024,2048]{1,0:T(8,128)(2,1)}) %all-gather.14.cloned.1.call-update) | async-done | bytes 4194320 | tf_op jit(solution)/shard_map/all_gather | solution.py:187
  522.5 7.6 fusion.47
  536.3 183.4 %all-gather.24.cloned.1.call-done = bf16[2048,8192]{1,0:T(8,128)(2,1)} async-done(((bf16[64,8192]{1,0:T(8,128)(2,1)}), bf16[2048,8192]{1,0:T(8,128)(2,1)}) %all-gather.24.cloned.1.call-update) | async-done | bytes 33554448 | tf_op jit(solution)/shard_map/all_gather | solution.py:166
  719.6 16.8 multiply_convert_fusion.5
  736.4 179.6 %all-gather.26.cloned.1.call-done = bf16[8192,2048]{1,0:T(8,128)(2,1)} async-done(((bf16[256,2048]{1,0:T(8,128)(2,1)}), bf16[8192,2048]{1,0:T(8,128)(2,1)}) %all-gather.26.cloned.1.call-update) | async-done | bytes 33554448 | tf_op jit(solution)/shard_map/all_gather | solution.py:168
  916.0 13.7 fusion.97
  930.0 16.1 multiply_convert_fusion.4
  946.1 14.0 fusion.98
  964.4 19.2 fusion.10
  983.6 19.7 multiply_reduce_fusion.3
  1003.3 18.8 fusion.17
  1022.1 19.9 fusion.90
  1051.7 8.1 convolution_convert_fusion
  1059.8 6.5 copy.77
  1073.0 8.2 convolution_convert_fusion.1
  1081.1 6.5 copy.73
  1088.2 8.3 multiply_reduce_fusion
  1104.7 6.5 copy.75
  1111.5 8.3 multiply_reduce_fusion.1
  1128.2 6.5 copy.71
  1152.9 12.2 reduce-scatter.33.cloned.1.call-done
  1169.7 9.3 fusion.71
  1179.2 9.7 fusion.57
  1188.9 26.6 reduce-scatter.35.cloned.1.call-done
  1217.6 48.3 %reduce-scatter.31.cloned.1.call-done = bf16[128,2048]{1,0:T(8,128)(2,1)} async-done(((bf16[1024,2048]{1,0:T(8,128)(2,1)}), bf16[128,2048]{1,0:T(8,128)(2,1)}) %reduce-scatter.31.cloned.1.call-update) | async-done | bytes 524304
  1267.9 9.3 fusion.53
  1277.3 9.3 fusion.70
  1287.8 24.9 fusion.34
  1314.5 25.0 fusion.26
  1342.6 6.5 convolution_add_fusion.8
  1349.1 6.5 convolution_add_fusion.11
  1368.8 26.5 all-reduce.21.cloned.1.call-done
  1406.7 179.1 %reduce-scatter.19.cloned.1.call-done = f32[64,2048]{1,0:T(8,128)} async-done(((f32[2048,2048]{1,0:T(8,128)}), f32[64,2048]{1,0:T(8,128)}) %reduce-scatter.19.cloned.1.call-update) | async-done | bytes 524304 | tf_op jit(solution)/shard_map/reduce_scatter | solution.py:311
  1585.8 187.2 %reduce-scatter.25.cloned.1.call-done = f32[64,2048]{1,0:T(8,128)} async-done(((f32[2048,2048]{1,0:T(8,128)}), f32[64,2048]{1,0:T(8,128)}) %reduce-scatter.25.cloned.1.call-update) | async-done | bytes 524304 | tf_op jit(solution)/shard_map/reduce_scatter | solution.py:316
  1773.0 187.2 %reduce-scatter.21.cloned.1.call-done = f32[64,2048]{1,0:T(8,128)} async-done(((f32[2048,2048]{1,0:T(8,128)}), f32[64,2048]{1,0:T(8,128)}) %reduce-scatter.21.cloned.1.call-update) | async-done | bytes 524304 | tf_op jit(solution)/shard_map/reduce_scatter | solution.py:313
  1960.2 187.3 %reduce-scatter.23.cloned.1.call-done = f32[64,2048]{1,0:T(8,128)} async-done(((f32[2048,2048]{1,0:T(8,128)}), f32[64,2048]{1,0:T(8,128)}) %reduce-scatter.23.cloned.1.call-update) | async-done | bytes 524304 | tf_op jit(solution)/shard_map/reduce_scatter | solution.py:314
  2147.6 710.0 %reduce-scatter.27.cloned.1.call-done = f32[64,8192]{1,0:T(8,128)} async-done(((f32[2048,8192]{1,0:T(8,128)}), f32[64,8192]{1,0:T(8,128)}) %reduce-scatter.27.cloned.1.call-update) | async-done | bytes 2097168 | tf_op jit(solution)/shard_map/reduce_scatter | solution.py:320
  2857.6 709.0 %reduce-scatter.29.cloned.1.call-done = f32[256,2048]{1,0:T(8,128)} async-done(((f32[8192,2048]{1,0:T(8,128)}), f32[256,2048]{1,0:T(8,128)}) %reduce-scatter.29.cloned.1.call-update) | async-done | bytes 2097168 | tf_op jit(solution)/shard_map/reduce_scatter | solution.py:322
  (298 shorter events, 179.9 us)
Async XLA Ops:
  7.2 84.5 %all-gather.18.cloned.1.call-start = ((), (), s32[]{:S(2)}) async-start(), calls=%async_computation.13 | async-start | bytes 8650752 | tf_op jit(solution)/shard_map/all_gather | solution.py:159
  9.0 162.3 %all-gather.12.cloned.1.call-start = ((), (), s32[]{:S(2)}) async-start(), calls=%async_computation.10 | async-start | bytes 8650752 | tf_op jit(solution)/shard_map/all_gather | solution.py:160
  10.9 240.3 %all-gather.16.cloned.1.call-start = ((), (), s32[]{:S(2)}) async-start(), calls=%async_computation.12 | async-start | bytes 8650752 | tf_op jit(solution)/shard_map/all_gather | solution.py:157
  12.7 286.2 %all-gather.20.cloned.1.call-start = ((), (), s32[]{:S(2)}) async-start(), calls=%async_computation.14 | async-start | bytes 4718592 | tf_op jit(solution)/shard_map/all_gather | solution.py:186
  14.5 236.7 %copy-start.2 = (bf16[128,2048]{1,0:T(8,128)(2,1)}, bf16[128,2048]{1,0:T(8,128)(2,1)S(1)}, u32[]{:S(2)}) copy-start(bf16[128,2048]{1,0:T(8,128)(2,1)S(1)} %get-tuple-element.96) | copy-start | bytes 1572868
  14.5 242.3 %copy-start.4 = (bf16[128,2048]{1,0:T(8,128)(2,1)}, bf16[128,2048]{1,0:T(8,128)(2,1)S(1)}, u32[]{:S(2)}) copy-start(bf16[128,2048]{1,0:T(8,128)(2,1)S(1)} %get-tuple-element.97) | copy-start | bytes 1572868
  97.2 249.7 %all-gather.30.cloned.1.call-start = ((), (), s32[]{:S(2)}) async-start(), calls=%async_computation.19 | async-start | bytes 4718592 | tf_op jit(solution)/shard_map/all_gather | solution.py:186
  97.3 5.7 copy-start.56
  97.3 5.7 copy-start.57
  97.3 5.7 copy-start.58
  102.8 292.0 %all-gather.28.cloned.1.call-start = ((), (), s32[]{:S(2)}) async-start(), calls=%async_computation.18 | async-start | bytes 4718592 | tf_op jit(solution)/shard_map/all_gather | solution.py:187
  145.0 31.8 copy-start.48
  176.8 297.7 %all-gather.22.cloned.1.call-start = ((), (), s32[]{:S(2)}) async-start(), calls=%async_computation.15 | async-start | bytes 8650752 | tf_op jit(solution)/shard_map/all_gather | solution.py:162
  177.6 5.7 copy-start.43
  177.6 344.9 %all-gather.14.cloned.1.call-start = ((), (), s32[]{:S(2)}) async-start(), calls=%async_computation.11 | async-start | bytes 4718592 | tf_op jit(solution)/shard_map/all_gather | solution.py:187
  183.3 54.3 %copy-start.49 = (s32[2,1,1024]{2,1,0:T(1,128)S(1)}, s32[2,1,1024]{2,1,0:T(1,128)}, u32[]{:S(2)}) copy-start(s32[2,1,1024]{2,1,0:T(1,128)} %param.19) | copy-start | bytes 24580
  183.3 536.4 %all-gather.24.cloned.1.call-start = ((), (), s32[]{:S(2)}) async-start(), calls=%async_computation.16 | async-start | bytes 34603008 | tf_op jit(solution)/shard_map/all_gather | solution.py:166
  184.4 731.6 %all-gather.26.cloned.1.call-start = ((), (), s32[]{:S(2)}) async-start(), calls=%async_computation.17 | async-start | bytes 34603008 | tf_op jit(solution)/shard_map/all_gather | solution.py:168
  187.2 963.6 %reduce-scatter.37.cloned.1.call-start = ((), (), s32[]{:S(2)}) async-start(), calls=%async_computation.29 | async-start | bytes 4718592
  262.1 91.2 %copy-start.28 = (bf16[128,2048]{0,1:T(8,128)(2,1)}, bf16[128,2048]{0,1:T(8,128)(2,1)S(1)}, u32[]{:S(2)}) copy-start(bf16[128,2048]{0,1:T(8,128)(2,1)S(1)} %copy.81) | copy-start | bytes 1572868
  360.9 113.6 %copy-start.24 = (f32[2,1,128,2048]{3,2,1,0:T(8,128)S(1)}, f32[2,1,128,2048]{3,2,1,0:T(8,128)}, u32[]{:S(2)}) copy-start(f32[2,1,128,2048]{3,2,1,0:T(8,128)} %param.18) | copy-start | bytes 6291460
  522.5 7.6 copy-start.25
  536.2 200.2 %copy-start.39 = (bf16[128,2048]{1,0:T(8,128)(2,1)}, bf16[128,2048]{1,0:T(8,128)(2,1)S(1)}, u32[]{:S(2)}) copy-start(bf16[128,2048]{1,0:T(8,128)(2,1)S(1)} %get-tuple-element.100) | copy-start | bytes 1572868
  536.2 393.7 %copy-start.41 = (bf16[128,2048]{1,0:T(8,128)(2,1)}, bf16[128,2048]{1,0:T(8,128)(2,1)S(1)}, u32[]{:S(2)}) copy-start(bf16[128,2048]{1,0:T(8,128)(2,1)S(1)} %get-tuple-element.101) | copy-start | bytes 1572868
  946.1 14.0 copy-start.17
  946.1 14.3 copy-start.8
  964.4 19.2 copy-start.20
  964.4 38.9 %copy-start.22 = (bf16[128,2048]{1,0:T(8,128)(2,1)}, bf16[128,2048]{1,0:T(8,128)(2,1)S(1)}, u32[]{:S(2)}) copy-start(bf16[128,2048]{1,0:T(8,128)(2,1)S(1)} %get-tuple-element.94) | copy-start | bytes 1572868
  1042.0 96.9 %copy-start.18 = (bf16[128,2048]{1,0:T(8,128)(2,1)}, bf16[128,2048]{1,0:T(8,128)(2,1)S(1)}, u32[]{:S(2)}) copy-start(bf16[128,2048]{1,0:T(8,128)(2,1)S(1)} %get-tuple-element.86) | copy-start | bytes 1572868
  1045.0 93.9 %copy-start.19 = (bf16[128,2048]{1,0:T(8,128)(2,1)}, bf16[128,2048]{1,0:T(8,128)(2,1)S(1)}, u32[]{:S(2)}) copy-start(bf16[128,2048]{1,0:T(8,128)(2,1)S(1)} %get-tuple-element.90) | copy-start | bytes 1572868
  1066.4 98.7 %reduce-scatter.33.cloned.1.call-start = ((), (), s32[]{:S(2)}) async-start(), calls=%async_computation.27 | async-start | bytes 4718592
  1087.7 127.8 %reduce-scatter.35.cloned.1.call-start = ((), (), s32[]{:S(2)}) async-start(), calls=%async_computation.28 | async-start | bytes 4718592
  1111.3 154.6 %reduce-scatter.31.cloned.1.call-start = ((), (), s32[]{:S(2)}) async-start(), calls=%async_computation.26 | async-start | bytes 4718592
  1134.8 260.5 %all-reduce.21.cloned.1.call-start = ((), (), s32[]{:S(2)}) async-start(), calls=%async_computation.30 | async-start | bytes 196608
  1148.6 21.1 copy-start.3
  1148.6 21.1 copy-start.5
  1169.3 416.5 %reduce-scatter.19.cloned.1.call-start = ((), (), s32[]{:S(2)}) async-start(), calls=%async_computation.20 | async-start | bytes 17301504 | tf_op jit(solution)/shard_map/reduce_scatter | solution.py:311
  1179.1 593.9 %reduce-scatter.25.cloned.1.call-start = ((), (), s32[]{:S(2)}) async-start(), calls=%async_computation.23 | async-start | bytes 17301504 | tf_op jit(solution)/shard_map/reduce_scatter | solution.py:316
  1188.8 771.4 %reduce-scatter.21.cloned.1.call-start = ((), (), s32[]{:S(2)}) async-start(), calls=%async_computation.21 | async-start | bytes 17301504 | tf_op jit(solution)/shard_map/reduce_scatter | solution.py:313
  1277.3 870.3 %reduce-scatter.23.cloned.1.call-start = ((), (), s32[]{:S(2)}) async-start(), calls=%async_computation.22 | async-start | bytes 17301504 | tf_op jit(solution)/shard_map/reduce_scatter | solution.py:314
  1286.7 1570.9 %reduce-scatter.27.cloned.1.call-start = ((), (), s32[]{:S(2)}) async-start(), calls=%async_computation.24 | async-start | bytes 69206016 | tf_op jit(solution)/shard_map/reduce_scatter | solution.py:320
  1312.7 2253.9 %reduce-scatter.29.cloned.1.call-start = ((), (), s32[]{:S(2)}) async-start(), calls=%async_computation.25 | async-start | bytes 69206016 | tf_op jit(solution)/shard_map/reduce_scatter | solution.py:322
  1342.6 6.5 copy-start.31
  1342.6 6.5 copy-start.36
  1342.6 13.0 slice-start.2
  1349.1 6.6 slice-start.3
  1349.1 6.5 copy-start.46
  1349.1 9.5 slice-start
  (36 other events, 122.9 us)
Sparse Core Ops, SparseCore 0:
  11.6 80.0 all-gather.17
  95.3 76.0 all-gather.11
  174.9 76.2 all-gather.15
  253.2 45.7 all-gather.19
  301.0 45.8 all-gather.29
  348.9 45.8 all-gather.27
  398.4 76.1 all-gather.21
  476.7 45.7 all-gather.13
  526.0 193.5 all-gather.23
  723.0 192.9 all-gather.25
  1066.5 48.1 reduce-scatter.36
  1116.9 48.1 reduce-scatter.32
  1167.4 48.1 reduce-scatter.34
  1217.7 48.1 reduce-scatter.30
  1272.1 123.1 all-reduce.20
  1398.1 187.6 reduce-scatter.18
  1588.6 184.3 reduce-scatter.24
  1775.8 184.3 reduce-scatter.20
  1963.2 184.3 reduce-scatter.22
  2150.5 707.0 reduce-scatter.26
  2860.6 705.9 reduce-scatter.28
where the time goes:
time: 3580 us; the launch traced here: 3570 us
  waiting for transfers between devices  2970 us (83%)
  matrix products  372 us (10%)
  blocking collectives  90.2 us (3%)
  local copies, waits for them, and re-layouts  73.9 us (2%)
  other arithmetic  45.7 us (1%)
    reduce_scatter x1, waiting for transfers between devices, shards(): lax.psum_scatter(terms[9], ('seq', 'fsdp'), scatter_dimension=0, tiled=True)  710 us
    reduce_scatter x1, waiting for transfers between devices, shards(): lax.psum_scatter(terms[11], ('seq', 'fsdp'), scatter_dimension=0, tiled=T...  709 us
    reduce_scatter x1, waiting for transfers between devices, shards(): lax.psum_scatter(terms[3], ('seq', 'fsdp'), scatter_dimension=0, tiled=True)  187 us
    reduce_scatter x1, waiting for transfers between devices, shards(): lax.psum_scatter(terms[2], ('seq', 'fsdp'), scatter_dimension=0, tiled=True)  187 us
    reduce_scatter x1, waiting for transfers between devices, shards(): lax.psum_scatter(terms[5], ('seq', 'fsdp'), scatter_dimension=0, tiled=True)  187 us
    all_gather x1, waiting for transfers between devices, shards(): lax.all_gather(local[9], ('seq', 'fsdp'), axis=0, tiled=True)  183 us
    all_gather x1, waiting for transfers between devices, shards(): lax.all_gather(local[11], ('seq', 'fsdp'), axis=0, tiled=True)  180 us
    reduce_scatter x1, waiting for transfers between devices, shards(): lax.psum_scatter(terms[0], ('seq', 'fsdp'), scatter_dimension=0, tiled=True)  179 us
  transfers between devices with their start and end apart: 21, of which 20 were waited for; matrix products, arithmetic and copies ran while one was open for 9% of the time, Pallas kernels for 0%

commit v1 on v0

--- a/solution.py
+++ b/solution.py
@@ -182,8 +182,33 @@
         value_rows = (matmul(rounded_in, value_matrix) + value_offset.astype(wide_type)).astype(
             low_type
         )
+
+        def time_kinds(tile_in, dev_axis):
+            response = lax.axis_size(dev_axis)
+            e_now = lax.axis_index(dev_axis)
+            part_next, front, after = (response, e_now, tile_in.shape[0])
+            block_list = list(map(lambda at: (at, (at + 1) % part_next), range(part_next)))
+            so_far_all = list(map(lambda at: (at, (at - 1) % part_next), range(part_next)))
+            v_next = jnp.zeros(
+                (*tile_in.shape[:0], part_next * after, *tile_in.shape[1:]), tile_in.dtype
+            )
+            v_next = lax.dynamic_update_slice_in_dim(v_next, tile_in, front * after, axis=0)
+            right_arr = item_now = tile_in
+            a_next = part_next // 2
+            for ix in tuple(range(1, a_next + 1)):
+                right_arr = lax.ppermute(right_arr, axis_name=dev_axis, perm=block_list)
+                v_next = lax.dynamic_update_slice_in_dim(
+                    v_next, right_arr, (front - ix) % part_next * after, axis=0
+                )
+                if ix < part_next - a_next:
+                    item_now = lax.ppermute(item_now, axis_name=dev_axis, perm=so_far_all)
+                    v_next = lax.dynamic_update_slice_in_dim(
+                        v_next, item_now, (front + ix) % part_next * after, axis=0
+                    )
+            return v_next
+
         key_whole, value_whole = (
-            lax.all_gather(key_rows, "fsdp", axis=0, tiled=True),
+            time_kinds(key_rows, "fsdp"),
             lax.all_gather(value_rows, "fsdp", axis=0, tiled=True),
         )
         length = key_whole.shape[0]

time: 3580 us -> 3520 us (0.983)
  waiting for transfers between devices: 2970 us -> 2880 us
    all_gather x2 -> x0, waiting for transfers between devices: 78.4 us -> none  [shards(): lax.all_gather(key_rows, 'fsdp', axis=0, tiled=True)]
    ppermute x0 -> x14, waiting for transfers between devices: none -> 61.9 us  [the longest x8 51.9 us: time_kinds(): right_arr = lax.ppermute(right_arr, axis_name=dev_axis, perm=block_list)]
    all_gather x1, waiting for transfers between devices: 13.3 us -> 69.1 us  [shards(): lax.all_gather(local[0], ('seq', 'fsdp'), axis=0, tiled=True)]
    all_gather x1, waiting for transfers between devices: 77.2 us -> 23.5 us  [shards(): lax.all_gather(local[2], ('seq', 'fsdp'), axis=0, tiled=True)]
    all_gather x1, waiting for transfers between devices: 71.5 us -> 18.7 us  [shards(): lax.all_gather(local[5], ('seq', 'fsdp'), axis=0, tiled=True)]
    unnamed x26 -> x24, waiting for transfers between devices: 114 us -> 113 us
  transfers between devices with their start and end apart: 21 -> 33, of which waited for: 20 -> 23; matrix products, arithmetic and copies ran while one was open for 9% -> 10% of each run, Pallas kernels for 0% -> 0%
where the time goes in v1:
time: 3520 us; the launch traced here: 3510 us
  waiting for transfers between devices  2880 us (82%)
  matrix products  367 us (10%)
  local copies, waits for them, and re-layouts  95.4 us (3%)
  blocking collectives  82.3 us (2%)
  other arithmetic  51.2 us (1%)
    reduce_scatter x1, waiting for transfers between devices, shards(): lax.psum_scatter(terms[9], ('seq', 'fsdp'), scatter_dimension=0, tiled=True)  710 us
    reduce_scatter x1, waiting for transfers between devices, shards(): lax.psum_scatter(terms[11], ('seq', 'fsdp'), scatter_dimension=0, tiled=T...  709 us
    reduce_scatter x1, waiting for transfers between devices, shards(): lax.psum_scatter(terms[2], ('seq', 'fsdp'), scatter_dimension=0, tiled=True)  187 us
    reduce_scatter x1, waiting for transfers between devices, shards(): lax.psum_scatter(terms[3], ('seq', 'fsdp'), scatter_dimension=0, tiled=True)  187 us
    reduce_scatter x1, waiting for transfers between devices, shards(): lax.psum_scatter(terms[5], ('seq', 'fsdp'), scatter_dimension=0, tiled=True)  187 us
    all_gather x1, waiting for transfers between devices, shards(): lax.all_gather(local[9], ('seq', 'fsdp'), axis=0, tiled=True)  183 us
    all_gather x1, waiting for transfers between devices, shards(): lax.all_gather(local[11], ('seq', 'fsdp'), axis=0, tiled=True)  180 us
    reduce_scatter x1, waiting for transfers between devices, shards(): lax.psum_scatter(terms[0], ('seq', 'fsdp'), scatter_dimension=0, tiled=True)  179 us
  transfers between devices with their start and end apart: 33, of which 23 were waited for; matrix products, arithmetic and copies ran while one was open for 10% of the time, Pallas kernels for 0%

profile of v1, /device:TPU:0, one launch (start us, length us, event | category | flops | bytes accessed | tf_op | source)
XLA Modules:
  0.0 3507.8 jit_solution(1484723465264510951)
XLA Ops:
  19.8 42.9 %all-reduce.18 = (bf16[2048]{0:T(1024)(128)(2,1)S(1)}, bf16[2048]{0:T(1024)(128)(2,1)S(1)}, bf16[2048]{0:T(1024)(128)(2,1)S(1)}, bf16[2048]{0:T(1024)(128)(2,1)S...) all-reduce(bf16[2048]{0:T(1024)(128)(2,1)S(1)} %dynamic-update-slic, ...), channel_id=1, replica_groups=mesh['seq'=4,'fsdp'=8] {'seq','fsdp'}, use_global_device_ids=true, to_apply=%add | all-reduce | flops 16384 | bytes 65536
  64.4 27.4 all-gather.10.cloned.1.call-done
  108.0 39.4 %all-gather = bf16[32,1,256]{2,1,0:T(2,128)(2,1)S(1)} all-gather(bf16[1,1,256]{2,1,0:T(2,128)(2,1)S(1)} %reshape.277), channel_id=1, replica_groups=mesh['seq'=4,'fsdp'=8] {'seq','fsdp'}, dimensions={0}, use_global_device_ids=true | all-gather | bytes 16896 | tf_op jit(solution)/shard_map/all_gather | solution.py:167
  148.0 23.5 all-gather.16.cloned.1.call-done
  185.3 69.1 %all-gather.14.cloned.1.call-done = bf16[2048,2048]{1,0:T(8,128)(2,1)} async-done(((bf16[64,2048]{1,0:T(8,128)(2,1)}), bf16[2048,2048]{1,0:T(8,128)(2,1)}) %all-gather.14.cloned.1.call-update) | async-done | bytes 8388624 | tf_op jit(solution)/shard_map/all_gather | solution.py:157
  282.4 14.1 collective-permute-done.9
  297.9 21.1 collective-permute-done.2
  330.7 9.8 collective-permute-done.4
  345.2 10.0 collective-permute-done.5
  382.7 7.5 fusion.47
  390.2 18.7 all-gather.18.cloned.1.call-done
  414.2 42.6 %all-gather.24.cloned.1.call-done = bf16[1024,2048]{1,0:T(8,128)(2,1)} async-done(((bf16[128,2048]{1,0:T(8,128)(2,1)}), bf16[1024,2048]{1,0:T(8,128)(2,1)}) %all-gather.24.cloned.1.call-update) | async-done | bytes 4194320 | tf_op jit(solution)/shard_map/all_gather | solution.py:212
  456.8 7.6 fusion.50
  470.6 183.3 %all-gather.20.cloned.1.call-done = bf16[2048,8192]{1,0:T(8,128)(2,1)} async-done(((bf16[64,8192]{1,0:T(8,128)(2,1)}), bf16[2048,8192]{1,0:T(8,128)(2,1)}) %all-gather.20.cloned.1.call-update) | async-done | bytes 33554448 | tf_op jit(solution)/shard_map/all_gather | solution.py:166
  653.9 16.9 multiply_convert_fusion.5
  670.9 179.6 %all-gather.22.cloned.1.call-done = bf16[8192,2048]{1,0:T(8,128)(2,1)} async-done(((bf16[256,2048]{1,0:T(8,128)(2,1)}), bf16[8192,2048]{1,0:T(8,128)(2,1)}) %all-gather.22.cloned.1.call-update) | async-done | bytes 33554448 | tf_op jit(solution)/shard_map/all_gather | solution.py:168
  850.5 13.7 fusion.99
  864.4 15.8 multiply_convert_fusion.4
  880.2 14.2 fusion.100
  898.7 19.2 fusion.10
  917.9 19.5 multiply_reduce_fusion.3
  937.4 18.8 fusion.17
  956.2 20.1 fusion.92
  986.0 8.1 convolution_convert_fusion
  994.1 6.5 copy.107
  1007.4 8.1 convolution_convert_fusion.1
  1015.5 6.5 copy.103
  1022.1 8.3 multiply_reduce_fusion
  1038.5 6.5 copy.105
  1045.5 8.3 multiply_reduce_fusion.1
  1062.3 6.6 copy.101
  1088.3 11.0 reduce-scatter.33.cloned.1.call-done
  1103.8 9.3 fusion.71
  1113.2 9.7 fusion.57
  1122.9 26.9 reduce-scatter.35.cloned.1.call-done
  1151.8 48.3 %reduce-scatter.31.cloned.1.call-done = bf16[128,2048]{1,0:T(8,128)(2,1)} async-done(((bf16[1024,2048]{1,0:T(8,128)(2,1)}), bf16[128,2048]{1,0:T(8,128)(2,1)}) %reduce-scatter.31.cloned.1.call-update) | async-done | bytes 524304
  1202.2 9.3 fusion.53
  1211.6 9.3 fusion.70
  1222.1 24.9 fusion.34
  1248.8 25.1 fusion.26
  1283.4 6.5 convolution_add_fusion.11
  1303.1 26.6 all-reduce.21.cloned.1.call-done
  1341.1 179.1 %reduce-scatter.19.cloned.1.call-done = f32[64,2048]{1,0:T(8,128)} async-done(((f32[2048,2048]{1,0:T(8,128)}), f32[64,2048]{1,0:T(8,128)}) %reduce-scatter.19.cloned.1.call-update) | async-done | bytes 524304 | tf_op jit(solution)/shard_map/reduce_scatter | solution.py:336
  1520.2 187.2 %reduce-scatter.25.cloned.1.call-done = f32[64,2048]{1,0:T(8,128)} async-done(((f32[2048,2048]{1,0:T(8,128)}), f32[64,2048]{1,0:T(8,128)}) %reduce-scatter.25.cloned.1.call-update) | async-done | bytes 524304 | tf_op jit(solution)/shard_map/reduce_scatter | solution.py:341
  1707.4 187.2 %reduce-scatter.21.cloned.1.call-done = f32[64,2048]{1,0:T(8,128)} async-done(((f32[2048,2048]{1,0:T(8,128)}), f32[64,2048]{1,0:T(8,128)}) %reduce-scatter.21.cloned.1.call-update) | async-done | bytes 524304 | tf_op jit(solution)/shard_map/reduce_scatter | solution.py:338
  1894.7 187.2 %reduce-scatter.23.cloned.1.call-done = f32[64,2048]{1,0:T(8,128)} async-done(((f32[2048,2048]{1,0:T(8,128)}), f32[64,2048]{1,0:T(8,128)}) %reduce-scatter.23.cloned.1.call-update) | async-done | bytes 524304 | tf_op jit(solution)/shard_map/reduce_scatter | solution.py:339
  2081.9 710.0 %reduce-scatter.27.cloned.1.call-done = f32[64,8192]{1,0:T(8,128)} async-done(((f32[2048,8192]{1,0:T(8,128)}), f32[64,8192]{1,0:T(8,128)}) %reduce-scatter.27.cloned.1.call-update) | async-done | bytes 2097168 | tf_op jit(solution)/shard_map/reduce_scatter | solution.py:345
  2791.9 709.0 %reduce-scatter.29.cloned.1.call-done = f32[256,2048]{1,0:T(8,128)} async-done(((f32[8192,2048]{1,0:T(8,128)}), f32[256,2048]{1,0:T(8,128)}) %reduce-scatter.29.cloned.1.call-update) | async-done | bytes 2097168 | tf_op jit(solution)/shard_map/reduce_scatter | solution.py:347
  (336 shorter events, 231.7 us)
Async XLA Ops:
  7.2 84.7 %all-gather.10.cloned.1.call-start = ((), (), s32[]{:S(2)}) async-start(), calls=%async_computation.10 | async-start | bytes 8650752 | tf_op jit(solution)/shard_map/all_gather | solution.py:160
  9.0 162.4 %all-gather.16.cloned.1.call-start = ((), (), s32[]{:S(2)}) async-start(), calls=%async_computation.13 | async-start | bytes 8650752 | tf_op jit(solution)/shard_map/all_gather | solution.py:159
  10.9 243.4 %all-gather.14.cloned.1.call-start = ((), (), s32[]{:S(2)}) async-start(), calls=%async_computation.12 | async-start | bytes 8650752 | tf_op jit(solution)/shard_map/all_gather | solution.py:157
  12.7 369.9 %all-gather.12.cloned.1.call-start = ((), (), s32[]{:S(2)}) async-start(), calls=%async_computation.11 | async-start | bytes 4718592 | tf_op jit(solution)/shard_map/all_gather | solution.py:212
  64.4 189.9 %copy-start.6 = (bf16[128,2048]{1,0:T(8,128)(2,1)}, bf16[128,2048]{1,0:T(8,128)(2,1)S(1)}, u32[]{:S(2)}) copy-start(bf16[128,2048]{1,0:T(8,128)(2,1)S(1)} %get-tuple-element.97) | copy-start | bytes 1572868
  64.4 194.7 %copy-start.4 = (bf16[128,2048]{1,0:T(8,128)(2,1)}, bf16[128,2048]{1,0:T(8,128)(2,1)S(1)}, u32[]{:S(2)}) copy-start(bf16[128,2048]{1,0:T(8,128)(2,1)S(1)} %get-tuple-element.96) | copy-start | bytes 1572868
  97.4 311.6 %all-gather.18.cloned.1.call-start = ((), (), s32[]{:S(2)}) async-start(), calls=%async_computation.14 | async-start | bytes 8650752 | tf_op jit(solution)/shard_map/all_gather | solution.py:162
  98.2 358.6 %all-gather.24.cloned.1.call-start = ((), (), s32[]{:S(2)}) async-start(), calls=%async_computation.17 | async-start | bytes 4718592 | tf_op jit(solution)/shard_map/all_gather | solution.py:212
  103.9 43.7 %copy-start.49 = (s32[2,1,1024]{2,1,0:T(1,128)S(1)}, s32[2,1,1024]{2,1,0:T(1,128)}, u32[]{:S(2)}) copy-start(s32[2,1,1024]{2,1,0:T(1,128)} %param.19) | copy-start | bytes 24580
  103.9 550.0 %all-gather.20.cloned.1.call-start = ((), (), s32[]{:S(2)}) async-start(), calls=%async_computation.15 | async-start | bytes 34603008 | tf_op jit(solution)/shard_map/all_gather | solution.py:166
  105.0 745.4 %all-gather.22.cloned.1.call-start = ((), (), s32[]{:S(2)}) async-start(), calls=%async_computation.16 | async-start | bytes 34603008 | tf_op jit(solution)/shard_map/all_gather | solution.py:168
  107.8 978.4 %reduce-scatter.37.cloned.1.call-start = ((), (), s32[]{:S(2)}) async-start(), calls=%async_computation.27 | async-start | bytes 4718592
  176.3 92.9 %collective-permute-start.7 = (bf16[128,2048]{1,0:T(8,128)(2,1)S(1)}, bf16[128,2048]{1,0:T(8,128)(2,1)}, u32[]{:S(2)}, u32[]{:S(2)}) collective-permute-start(bf16[128,2048]{1,0:T(8,128)(2,1)S(1)} %convolution_convert_fusion.4), channel_id=1, source_target_pairs={{0,1},{1,2},{2,3},{3,4},{4,5},{5,6},{6,7},{7,0},{8,9},{9,10},{10,1... | collective-permute-start | bytes 1572872 | tf_op jit(solution)/shard_map/ppermute | solution.py:199
  176.6 98.9 %collective-permute-start.8 = (bf16[128,2048]{1,0:T(8,128)(2,1)S(1)}, bf16[128,2048]{1,0:T(8,128)(2,1)}, u32[]{:S(2)}, u32[]{:S(2)}) collective-permute-start(bf16[128,2048]{1,0:T(8,128)(2,1)S(1)} %convolution_convert_fusion.4), channel_id=1, source_target_pairs={{0,7},{1,0},{2,1},{3,2},{4,3},{5,4},{6,5},{7,6},{8,15},{9,8},{10,9... | collective-permute-start | bytes 1572872 | tf_op jit(solution)/shard_map/ppermute | solution.py:204
  181.5 89.5 %collective-permute-start = (bf16[128,2048]{1,0:T(8,128)(2,1)S(1)}, bf16[128,2048]{1,0:T(8,128)(2,1)}, u32[]{:S(2)}, u32[]{:S(2)}) collective-permute-start(bf16[128,2048]{1,0:T(8,128)(2,1)S(1)} %convolution_convert_fusion.5), channel_id=1, source_target_pairs={{0,1},{1,2},{2,3},{3,4},{4,5},{5,6},{6,7},{7,0},{8,9},{9,10},{10,1... | collective-permute-start | bytes 1572872 | tf_op jit(solution)/shard_map/ppermute | solution.py:199
  181.5 97.6 %collective-permute-start.1 = (bf16[128,2048]{1,0:T(8,128)(2,1)S(1)}, bf16[128,2048]{1,0:T(8,128)(2,1)}, u32[]{:S(2)}, u32[]{:S(2)}) collective-permute-start(bf16[128,2048]{1,0:T(8,128)(2,1)S(1)} %convolution_convert_fusion.5), channel_id=1, source_target_pairs={{0,7},{1,0},{2,1},{3,2},{4,3},{5,4},{6,5},{7,6},{8,15},{9,8},{10,9... | collective-permute-start | bytes 1572872 | tf_op jit(solution)/shard_map/ppermute | solution.py:204
  268.8 98.9 %copy-start.25 = (bf16[128,2048]{0,1:T(8,128)(2,1)}, bf16[128,2048]{0,1:T(8,128)(2,1)S(1)}, u32[]{:S(2)}) copy-start(bf16[128,2048]{0,1:T(8,128)(2,1)S(1)} %copy.109) | copy-start | bytes 1572868
  269.1 106.2 %copy-start.27 = (bf16[128,2048]{0,1:T(8,128)(2,1)}, bf16[128,2048]{0,1:T(8,128)(2,1)S(1)}, u32[]{:S(2)}) copy-start(bf16[128,2048]{0,1:T(8,128)(2,1)S(1)} %copy.110) | copy-start | bytes 1572868
  270.7 25.9 collective-permute-start.9
  272.3 46.7 %collective-permute-start.2 = (bf16[128,2048]{1,0:T(8,128)(2,1)}, bf16[128,2048]{1,0:T(8,128)(2,1)}, u32[]{:S(2)}, u32[]{:S(2)}) collective-permute-start(bf16[128,2048]{1,0:T(8,128)(2,1)} %collective-permute-done), channel_id=1, source_target_pairs={{0,1},{1,2},{2,3},{3,4},{4,5},{5,6},{6,7},{7,0},{8,9},{9,10},{10,1... | collective-permute-start | bytes 1572872 | tf_op jit(solution)/shard_map/ppermute | solution.py:199
  276.8 45.4 %collective-permute-start.10 = (bf16[128,2048]{1,0:T(8,128)(2,1)}, bf16[128,2048]{1,0:T(8,128)(2,1)S(1)}, u32[]{:S(2)}, u32[]{:S(2)}) collective-permute-start(bf16[128,2048]{1,0:T(8,128)(2,1)} %collective-permute-done.8), channel_id=1, source_target_pairs={{0,7},{1,0},{2,1},{3,2},{4,3},{5,4},{6,5},{7,6},{8,15},{9,8},{10,9... | collective-permute-start | bytes 1572872 | tf_op jit(solution)/shard_map/ppermute | solution.py:204
  280.4 45.5 %collective-permute-start.3 = (bf16[128,2048]{1,0:T(8,128)(2,1)}, bf16[128,2048]{1,0:T(8,128)(2,1)S(1)}, u32[]{:S(2)}, u32[]{:S(2)}) collective-permute-start(bf16[128,2048]{1,0:T(8,128)(2,1)} %collective-permute-done.1), channel_id=1, source_target_pairs={{0,7},{1,0},{2,1},{3,2},{4,3},{5,4},{6,5},{7,6},{8,15},{9,8},{10,9... | collective-permute-start | bytes 1572872 | tf_op jit(solution)/shard_map/ppermute | solution.py:204
  297.9 31.4 collective-permute-start.11
  320.3 20.2 collective-permute-start.4
  322.5 21.4 collective-permute-start.12
  326.2 28.9 collective-permute-start.5
  330.6 27.7 collective-permute-start.13
  341.8 23.5 collective-permute-start.6
  390.2 23.7 copy-start.37
  470.6 200.2 %copy-start.39 = (bf16[128,2048]{1,0:T(8,128)(2,1)}, bf16[128,2048]{1,0:T(8,128)(2,1)S(1)}, u32[]{:S(2)}) copy-start(bf16[128,2048]{1,0:T(8,128)(2,1)S(1)} %get-tuple-element.100) | copy-start | bytes 1572868
  470.6 393.8 %copy-start.41 = (bf16[128,2048]{1,0:T(8,128)(2,1)}, bf16[128,2048]{1,0:T(8,128)(2,1)S(1)}, u32[]{:S(2)}) copy-start(bf16[128,2048]{1,0:T(8,128)(2,1)S(1)} %get-tuple-element.101) | copy-start | bytes 1572868
  880.2 14.5 copy-start.10
  898.7 19.2 copy-start.20
  898.7 38.7 %copy-start.22 = (bf16[128,2048]{1,0:T(8,128)(2,1)}, bf16[128,2048]{1,0:T(8,128)(2,1)S(1)}, u32[]{:S(2)}) copy-start(bf16[128,2048]{1,0:T(8,128)(2,1)S(1)} %get-tuple-element.94) | copy-start | bytes 1572868
  976.3 96.7 %copy-start.18 = (bf16[128,2048]{1,0:T(8,128)(2,1)}, bf16[128,2048]{1,0:T(8,128)(2,1)S(1)}, u32[]{:S(2)}) copy-start(bf16[128,2048]{1,0:T(8,128)(2,1)S(1)} %get-tuple-element.86) | copy-start | bytes 1572868
  979.3 93.7 %copy-start.19 = (bf16[128,2048]{1,0:T(8,128)(2,1)}, bf16[128,2048]{1,0:T(8,128)(2,1)S(1)}, u32[]{:S(2)}) copy-start(bf16[128,2048]{1,0:T(8,128)(2,1)S(1)} %get-tuple-element.90) | copy-start | bytes 1572868
  1000.7 98.7 %reduce-scatter.33.cloned.1.call-start = ((), (), s32[]{:S(2)}) async-start(), calls=%async_computation.25 | async-start | bytes 4718592
  1022.0 127.8 %reduce-scatter.35.cloned.1.call-start = ((), (), s32[]{:S(2)}) async-start(), calls=%async_computation.26 | async-start | bytes 4718592
  1045.1 155.0 %reduce-scatter.31.cloned.1.call-start = ((), (), s32[]{:S(2)}) async-start(), calls=%async_computation.24 | async-start | bytes 4718592
  1068.9 260.8 %all-reduce.21.cloned.1.call-start = ((), (), s32[]{:S(2)}) async-start(), calls=%async_computation.28 | async-start | bytes 196608
  1084.0 19.8 copy-start.5
  1084.0 19.8 copy-start.7
  1103.5 416.7 %reduce-scatter.19.cloned.1.call-start = ((), (), s32[]{:S(2)}) async-start(), calls=%async_computation.18 | async-start | bytes 17301504 | tf_op jit(solution)/shard_map/reduce_scatter | solution.py:336
  1113.1 594.3 %reduce-scatter.25.cloned.1.call-start = ((), (), s32[]{:S(2)}) async-start(), calls=%async_computation.21 | async-start | bytes 17301504 | tf_op jit(solution)/shard_map/reduce_scatter | solution.py:341
  1122.9 771.8 %reduce-scatter.21.cloned.1.call-start = ((), (), s32[]{:S(2)}) async-start(), calls=%async_computation.19 | async-start | bytes 17301504 | tf_op jit(solution)/shard_map/reduce_scatter | solution.py:338
  1211.5 870.4 %reduce-scatter.23.cloned.1.call-start = ((), (), s32[]{:S(2)}) async-start(), calls=%async_computation.20 | async-start | bytes 17301504 | tf_op jit(solution)/shard_map/reduce_scatter | solution.py:339
  1220.9 1571.0 %reduce-scatter.27.cloned.1.call-start = ((), (), s32[]{:S(2)}) async-start(), calls=%async_computation.22 | async-start | bytes 69206016 | tf_op jit(solution)/shard_map/reduce_scatter | solution.py:345
  1247.0 2253.9 %reduce-scatter.29.cloned.1.call-start = ((), (), s32[]{:S(2)}) async-start(), calls=%async_computation.23 | async-start | bytes 69206016 | tf_op jit(solution)/shard_map/reduce_scatter | solution.py:347
  (40 other events, 182.4 us)
Sparse Core Ops, SparseCore 0:
  11.6 80.2 all-gather.9
  95.4 76.0 all-gather.15
  175.0 79.2 all-gather.13
  256.3 62.4 all-gather.11
  322.3 86.6 all-gather.17
  411.0 45.7 all-gather.23
  460.4 193.4 all-gather.19
  657.5 192.9 all-gather.21
  1000.8 48.1 reduce-scatter.36
  1051.1 48.1 reduce-scatter.32
  1101.6 48.1 reduce-scatter.34
  1151.9 48.1 reduce-scatter.30
  1206.5 123.1 all-reduce.20
  1332.5 187.6 reduce-scatter.18
  1523.0 184.3 reduce-scatter.24
  1710.3 184.3 reduce-scatter.20
  1897.5 184.3 reduce-scatter.22
  2084.8 707.0 reduce-scatter.26
  2795.0 705.9 reduce-scatter.28
